TPU v7x, 32 devices: a whole 2x2x4 slice. The times are simulated.
32 devices in a mesh: dp: 2 (over x), hist: 16 (over z, y, core).
Axes of the slice: x: 2, y: 2, z: 4, core: 2. Of those that a mesh axis runs over, the one named last changes fastest.
Arguments:
- queries: bfloat16 [2, 8192, 512], P('dp', 'hist'), may hold values from -6 to 6
- key_rows: bfloat16 [2, 8192, 512], P('dp', 'hist'), may hold values from -6 to 6
- value_rows: bfloat16 [2, 8192, 512], P('dp', 'hist'), may hold values from -6 to 6
- gate_rows: bfloat16 [2, 8192, 512], P('dp', 'hist'), may hold values from -6 to 6
- user_start: int32 [2, 8192], P('dp', 'hist'), may hold values from 0 to 8191, as said below
- w_out: bfloat16 [512, 1024], replicated, may hold values from -0.25 to 0.25
- out_grad: bfloat16 [2, 8192, 1024], P('dp', 'hist'), may hold values from -6 to 6
Outputs:
- query_grad: bfloat16 [2, 8192, 512], P('dp', 'hist')
- key_grad: bfloat16 [2, 8192, 512], P('dp', 'hist')
- value_grad: bfloat16 [2, 8192, 512], P('dp', 'hist')
- gate_grad: bfloat16 [2, 8192, 512], P('dp', 'hist')
- weight_grad: float32 [512, 1024], P('hist')
Inputs may be any that keep to these rules, and one draw needn't show every extreme that they name: user_start[g, i] is the position within group g of the first event of event i's user: it is at most i, never falls along the events, equals i where a user begins, and is 0 at the first event; the last event of every group is a user of its own.
All inputs are finite; a program needn't handle non-finite values.
Results may differ from a plain program's by a relative error of at most 0.012.
Values may be sent and summed in bfloat16 or wider, within the bound.
A program may use at most 128 MiB of HBM per device.

v0:
```python
import math
import jax
import jax.numpy as jnp
from jax import lax
from jax.sharding import PartitionSpec as P

HEADS = 4
HS = 128
WIN = 512
EPSILON = 1e-05


def shifted(value, axis, steps):
    count = lax.axis_size(axis)
    first, last = (max(0, -steps), min(count, count - steps))
    return lax.ppermute(value, axis, [(source, source + steps) for source in range(first, last)])


def split_heads(values):
    return values.reshape(values.shape[0], HEADS, HS)


def score_block(query_rows, key_piece):
    product = jnp.einsum(
        "rhd,chd->hrc",
        split_heads(query_rows),
        split_heads(key_piece),
        preferred_element_type=jnp.float32,
    )
    return product * HS ** (-0.5)


def window_mask(query_pos, start_rows, key_pos):
    spacing = query_pos[:, None] - key_pos[None, :]
    return (key_pos[None, :] >= start_rows[:, None]) & (spacing >= 0) & (spacing < WIN)


def silu_weights(scaled, live_map):
    sigmoid_s = jax.nn.sigmoid(scaled)
    weights = jnp.where(live_map[None], scaled * sigmoid_s / WIN, 0.0).astype(jnp.bfloat16)
    return (sigmoid_s, weights)


def attend(query_rows, key_piece, value_piece, live_map):
    scaled = score_block(query_rows, key_piece)
    sigmoid_s, weights = silu_weights(scaled, live_map)
    mixed = jnp.einsum(
        "hrc,chd->rhd", weights, split_heads(value_piece), preferred_element_type=jnp.float32
    )
    return mixed.reshape(query_rows.shape[0], -1)


def back_piece(query_rows, d_attn, key_piece, value_piece, live_map, want_keys):
    inv_root = HS ** (-0.5)
    scaled = score_block(query_rows, key_piece)
    sigmoid_s, weights = silu_weights(scaled, live_map)
    d_weights = jnp.einsum(
        "rhd,chd->hrc",
        split_heads(d_attn),
        split_heads(value_piece),
        preferred_element_type=jnp.float32,
    )
    d_scores = jnp.where(
        live_map[None], d_weights * sigmoid_s * (1.0 + scaled * (1.0 - sigmoid_s)) / WIN, 0.0
    )
    d_scores = d_scores.astype(jnp.bfloat16)
    results = []
    query_part = jnp.einsum(
        "hrc,chd->rhd", d_scores, split_heads(key_piece), preferred_element_type=jnp.float32
    )
    results.append(query_part.reshape(query_rows.shape[0], -1) * inv_root)
    key_part = jnp.einsum(
        "hrc,rhd->chd", d_scores, split_heads(query_rows), preferred_element_type=jnp.float32
    )
    value_part = jnp.einsum(
        "hrc,rhd->chd", weights, split_heads(d_attn), preferred_element_type=jnp.float32
    )
    results.append(key_part.reshape(want_keys, -1) * inv_root)
    results.append(value_part.reshape(want_keys, -1))
    return tuple(results)


def row_section(attended, gate_blk, grad_blk, w_out):
    row_mean = jnp.mean(attended, axis=-1, keepdims=True)
    centred = attended - row_mean
    inverse = lax.rsqrt(jnp.mean(centred * centred, axis=-1, keepdims=True) + EPSILON)
    normed = centred * inverse
    gate_wide = gate_blk.astype(jnp.float32)
    hidden = (normed * gate_wide).astype(jnp.bfloat16)
    d_hidden = lax.dot_general(
        grad_blk, w_out, (((1,), (1,)), ((), ())), preferred_element_type=jnp.float32
    )
    gate_grad = (d_hidden * normed).astype(jnp.bfloat16)
    d_normed = d_hidden * gate_wide
    d_attn = inverse * (
        d_normed
        - jnp.mean(d_normed, axis=-1, keepdims=True)
        - normed * jnp.mean(d_normed * normed, axis=-1, keepdims=True)
    )
    return (hidden, gate_grad, d_attn.astype(jnp.bfloat16))


def shards(queries, key_rows, value_rows, gate_rows, user_start, w_out, out_grad):
    query_loc = queries[0]
    key_loc = key_rows[0]
    value_loc = value_rows[0]
    gate_loc = gate_rows[0]
    start_loc = user_start[0]
    grad_loc = out_grad[0]
    ev_rows = query_loc.shape[0]
    tail = min(WIN, ev_rows)
    reach = -(-WIN // ev_rows)
    index = lax.axis_index("hist")
    hist_size = lax.axis_size("hist")
    row_ids = jnp.arange(ev_rows, dtype=jnp.int32)
    query_pos = index * ev_rows + row_ids
    tail_ids = jnp.arange(tail, dtype=jnp.int32) + (ev_rows - tail)
    offset = 1
    got_keys, got_values = shifted((key_loc, value_loc), "hist", offset)
    halo_pieces = [(got_keys, got_values, (index - offset) * ev_rows + tail_ids)]
    halo_live = [window_mask(query_pos, start_loc, member[2]) for member in halo_pieces]
    local_live = window_mask(query_pos, start_loc, query_pos)
    key_all = jnp.concatenate([member[0] for member in halo_pieces] + [key_loc], 0)
    value_all = jnp.concatenate([member[1] for member in halo_pieces] + [value_loc], 0)
    live_all = jnp.concatenate(halo_live + [local_live], 1)
    attended = attend(query_loc, key_all, value_all, live_all)
    hidden, gate_grad, d_attn = row_section(attended, gate_loc, grad_loc, w_out)
    want_all = reach * tail + ev_rows
    query_part, key_part, value_part = back_piece(
        query_loc, d_attn, key_all, value_all, live_all, want_all
    )
    local_key = key_part[want_all - ev_rows :]
    local_value = value_part[want_all - ev_rows :]
    remote_parts = [(key_part[0:tail], value_part[0:tail])]
    offset = 1
    got_key, got_value = shifted(
        (remote_parts[offset - 1][0], remote_parts[offset - 1][1]), "hist", -offset
    )
    key_total = local_key + got_key
    value_total = local_value + got_value
    weight_part = lax.psum_scatter(
        lax.dot_general(
            hidden, grad_loc, (((0,), (0,)), ((), ())), preferred_element_type=jnp.float32
        ),
        "hist",
        scatter_dimension=0,
        tiled=True,
    )
    weight_total = lax.psum(weight_part.astype(jnp.bfloat16), "dp").astype(jnp.float32)
    total_rows = lax.axis_size("dp") * hist_size * ev_rows
    weight_grad = weight_total / math.sqrt(total_rows)
    return (
        query_part.astype(jnp.bfloat16)[None],
        key_total.astype(jnp.bfloat16)[None],
        value_total.astype(jnp.bfloat16)[None],
        gate_grad[None],
        weight_grad,
    )


def solution(mesh):
    return jax.shard_map(
        shards,
        mesh=mesh,
        in_specs=(
            P("dp", "hist", None),
            P("dp", "hist", None),
            P("dp", "hist", None),
            P("dp", "hist", None),
            P("dp", "hist"),
            P(),
            P("dp", "hist", None),
        ),
        out_specs=(
            P("dp", "hist", None),
            P("dp", "hist", None),
            P("dp", "hist", None),
            P("dp", "hist", None),
            P("hist", None),
        ),
        check_vma=False,
    )
```

profile of v0, /device:TPU:0, one launch (start us, length us, event | category | flops | bytes accessed | tf_op | source)
XLA Modules:
  0.0 138.0 jit_solution(251763052997868147)
XLA Ops:
  7.2 0.0 copy-start
  7.2 0.0 copy-start.6
  7.2 0.0 copy-start.9
  7.2 0.0 reduce-scatter.2.cloned.1.call-start
  7.2 1.4 copy.31
  8.6 3.2 %collective-permute-start = (bf16[512,512]{0,1:T(8,128)(2,1)S(1)}, bf16[512,512]{0,1:T(8,128)(2,1)}, u32[]{:S(2)}, u32[]{:S(2)}) collective-permute-start(bf16[512,512]{0,1:T(8,128)(2,1)S(1)} %bitcast.106), channel_id=1, source_target_pairs={{0,1},{1,2},{2,3},{3,4},{4,5},{5,6},{6,7},{7,8},{8,9},{9,10},{10,1... | collective-permute-start | bytes 1572872 | tf_op jit(solution)/shard_map/ppermute | solution.py:16
  11.8 4.5 %collective-permute-start.1 = (bf16[512,512]{1,0:T(8,128)(2,1)}, bf16[512,512]{1,0:T(8,128)(2,1)}, u32[]{:S(2)}, u32[]{:S(2)}) collective-permute-start(bf16[512,512]{1,0:T(8,128)(2,1)} %bitcast.113), channel_id=1, source_target_pairs={{0,1},{1,2},{2,3},{3,4},{4,5},{5,6},{6,7},{7,8},{8,9},{9,10},{10,1... | collective-permute-start | bytes 1572872 | tf_op jit(solution)/shard_map/ppermute | solution.py:16
  16.4 2.0 %copy.36 = bf16[1,512,512]{1,2,0:T(8,128)(2,1)} copy(bf16[1,512,512]{2,1,0:T(8,128)(2,1)} %param.9) | data formatting | bytes 1048576 | tf_op args[2]
  18.4 1.0 copy.34
  19.4 1.3 copy.62
  20.7 0.0 copy-done.6
  20.7 0.0 copy-start.4
  20.7 0.2 copy.39
  20.9 0.0 copy-done.9
  20.9 0.7 fusion.18
  21.6 0.8 pad_add_fusion
  22.4 0.0 collective-permute-done
  22.4 1.3 copy.33
  23.7 0.0 copy-start.8
  23.8 0.0 copy-start.7
  23.8 7.5 %fusion.5 = (bf16[4,512,1024]{1,2,0:T(8,128)(2,1)}, f32[4,1024,512]{2,1,0:T(8,128)}) fusion(pred[512,1024]{0,1:T(8,128)(4,1)} %pad_add_fusion, bf16[512,4,128]{0,2,1:T(8,128)(2,1)S(1)} %bitcast.111, bf16[512,4,128]{2,0,1:T(8,128)(2,1)} %copy.34, bf16[512,4,128]{2,0,1:T(8,128)(2,1)S(1)} %copy.33), kind=kOutput, calls=%fused_computation.8 | convolution fusion | flops 555745280 | bytes 14680064 | tf_op jit(solution)/shard_map/rhd,chd->hrc/dot_general | solution.py:24
  31.2 0.0 copy-done.4
  31.3 0.0 copy-done.8
  31.3 0.0 collective-permute-done.1
  31.3 2.0 %copy.35 = bf16[512,512]{0,1:T(8,128)(2,1)} copy(bf16[512,512]{1,0:T(8,128)(2,1)} %collective-permute-done.1) | data formatting | bytes 1048576 | tf_op jit(solution)/shard_map/ppermute | solution.py:16
  33.3 0.0 copy-done.7
  33.3 3.1 %fusion.32 = (f32[512]{0:T(512)S(1)}, f32[4,128,512]{2,1,0:T(8,128)S(1)}) fusion(bf16[4,512,1024]{1,2,0:T(8,128)(2,1)} %get-tuple-element.25, bf16[512,4,128]{0,2,1:T(8,128)(2,1)S(1)} %bitcast.115, bf16[512,4,128]{0,2,1:T(8,128)(2,1)} %bitcast.116), kind=kOutput, calls=%fused_computation.62 | convolution fusion | flops 539229696 | bytes 6293504 | tf_op jit(solution)/shard_map/hrc,chd->rhd/dot_general | solution.py:47
  36.4 0.2 multiply_reduce_fusion.1
  36.6 0.2 multiply_convert_fusion
  36.8 0.0 copy-done
  36.8 2.0 %fusion.13 = f32[512,1024]{1,0:T(8,128)} fusion(bf16[512,512]{0,1:T(8,128)(2,1)S(1)} %bitcast.108, bf16[1,512,1024]{2,1,0:T(8,128)(2,1)S(1)} %copy-done), kind=kOutput, calls=%fused_computation.28 | convolution fusion | flops 536870912 | bytes 3670016 | tf_op jit(solution)/shard_map/dot_general | solution.py:142
  38.8 0.0 reduce-scatter.2.cloned.1.call-update
  38.9 0.0 all-reduce.2.cloned.1.call-start
  38.9 0.0 copy-start.1
  38.9 2.2 %fusion.25 = (f32[512]{0:T(512)S(1)}, f32[512]{0:T(512)S(1)}, f32[512,512]{0,1:T(8,128)S(1)}) fusion(bf16[1,512,512]{1,2,0:T(8,128)(2,1)S(1)} %copy.39, f32[512]{0:T(512)S(1)} %add_rsqrt_fusion, f32[512]{0:T(512)S(1)} %broadcast_multiply_fusion.2, f32[4,128,512]{2,1,0:T(8,128)S(1)} %get-tuple-element.28, bf16[512,1024]{1,0:T(8,128)(2,1)} %param.12, ...), kind=kOutput, calls=%fused_computation.48 | convolution fusion | flops 538704896 | bytes 4726784 | tf_op jit(solution)/shard_map/dot_general | solution.py:90
  41.2 1.2 multiply_convert_fusion.1
  42.3 0.0 copy-done.1
  42.3 1.5 %convolution_bitcast_fusion = f32[1024,4,128]{0,2,1:T(8,128)S(1)} fusion(bf16[512,4,128]{0,2,1:T(8,128)(2,1)S(1)} %bitcast.109, bf16[4,512,1024]{1,2,0:T(8,128)(2,1)S(1)} %copy-done.1), kind=kOutput, calls=%fused_computation.16 | convolution fusion | flops 536870912 | bytes 6815744 | tf_op jit(solution)/shard_map/hrc,rhd->chd/dot_general | solution.py:75
  43.8 0.2 fusion.30
  44.0 0.0 copy-done.3
  44.0 1.4 %copy.50 = f32[512,512]{1,0:T(8,128)} copy(f32[512,512]{0,1:T(8,128)S(1)} %bitcast.103) | data formatting | bytes 2097152 | tf_op jit(solution)/shard_map/slice | solution.py:134
  45.5 1.5 %collective-permute-start.3 = (f32[512,512]{1,0:T(8,128)}, f32[512,512]{1,0:T(8,128)}, u32[]{:S(2)}, u32[]{:S(2)}) collective-permute-start(f32[512,512]{1,0:T(8,128)} %copy.50), channel_id=1, source_target_pairs={{1,0},{2,1},{3,2},{4,3},{5,4},{6,5},{7,6},{8,7},{9,8},{10,9},{11,1... | collective-permute-start | bytes 3145736 | tf_op jit(solution)/shard_map/ppermute | solution.py:16
  46.9 0.0 copy-start.5
  46.9 7.5 %fusion.10 = bf16[4,512,1024]{1,2,0:T(8,128)(2,1)S(1)} fusion(f32[4,1024,512]{2,1,0:T(8,128)} %get-tuple-element.26, pred[512,1024]{0,1:T(8,128)(4,1)} %pad_add_fusion, bf16[512,4,128]{0,2,1:T(8,128)(2,1)} %bitcast.110, bf16[512,4,128]{0,2,1:T(8,128)(2,1)} %bitcast.114, bf16[512,4,128]{0,2,1:T(8,128)(2,1)} %bitcast.117), kind=kOutput, calls=%fused_computation.13 | convolution fusion | flops 564133888 | bytes 14680064 | tf_op jit(solution)/shard_map/rhd,chd->hrc/dot_general | solution.py:57
  54.5 0.0 copy-done.5
  54.5 0.0 copy-start.2
  54.5 1.5 %multiply_bitcast_fusion = f32[1024,4,128]{0,2,1:T(8,128)S(1)} fusion(bf16[4,512,1024]{1,2,0:T(8,128)(2,1)S(1)} %fusion.10, bf16[512,4,128]{0,2,1:T(8,128)(2,1)S(1)} %bitcast.112), kind=kOutput, calls=%fused_computation.14 | convolution fusion | flops 537395200 | bytes 6815744 | tf_op jit(solution)/shard_map/hrc,rhd->chd/dot_general | solution.py:72
  56.0 1.1 fusion.31
  57.1 1.3 copy.47
  58.4 1.3 collective-permute-start.2
  59.7 0.3 copy.51
  60.1 1.6 %copy.48 = f32[512,512]{1,0:T(8,128)S(1)} copy(f32[512,512]{0,1:T(8,128)} %bitcast.102) | data formatting | bytes 2097152 | tf_op jit(solution)/shard_map/slice | solution.py:132
  61.6 4.1 %fusion.11 = bf16[4,128,512]{2,1,0:T(8,128)(2,1)} fusion(bf16[4,512,1024]{1,2,0:T(8,128)(2,1)} %copy-done.2, bf16[512,4,128]{2,0,1:T(8,128)(2,1)} %copy.34, bf16[512,4,128]{2,0,1:T(8,128)(2,1)} %copy-done.8), kind=kOutput, calls=%fused_computation.22 | convolution fusion | flops 539492352 | bytes 5767168 | tf_op jit(solution)/shard_map/hrc,chd->rhd/dot_general | solution.py:68
  65.8 2.1 %copy.52 = bf16[1,512,512]{2,1,0:T(8,128)(2,1)} copy(bf16[1,512,512]{1,2,0:T(8,128)(2,1)} %bitcast.118) | data formatting | bytes 1048576
  67.8 2.0 %copy.53 = bf16[1,512,512]{2,1,0:T(8,128)(2,1)} copy(bf16[1,512,512]{1,2,0:T(8,128)(2,1)} %bitcast.105) | data formatting | bytes 1048576
  69.9 0.0 collective-permute-done.3
  69.9 2.2 %fusion.24 = bf16[1,512,512]{2,1,0:T(8,128)(2,1)} fusion(f32[512,512]{1,0:T(8,128)S(1)} %copy.51, f32[512,512]{1,0:T(8,128)} %collective-permute-done.3), kind=kLoop, calls=%fused_computation.47 | loop fusion | flops 524288 | bytes 2621440 | tf_op jit(solution)/shard_map/broadcast_in_dim | solution.py:155
  72.0 34.9 %reduce-scatter.2.cloned.1.call-done = f32[32,1024]{1,0:T(8,128)} async-done(((f32[512,1024]{1,0:T(8,128)}), f32[32,1024]{1,0:T(8,128)}) %reduce-scatter.2.cloned.1.call-update) | async-done | bytes 131088 | tf_op jit(solution)/shard_map/reduce_scatter | solution.py:141
  106.9 1.5 %convert_element_type.74 = bf16[32,1024]{1,0:T(8,128)(2,1)} convert(f32[32,1024]{1,0:T(8,128)} %reduce-scatter.2.cloned.1.call-done) | non-fusion elementwise | flops 32768 | bytes 196608 | tf_op jit(solution)/shard_map/convert_element_type | solution.py:149
  108.5 0.0 all-reduce.2.cloned.1.call-update
  108.5 0.0 collective-permute-done.2
  108.5 2.2 %fusion.23 = bf16[1,512,512]{2,1,0:T(8,128)(2,1)} fusion(f32[512,512]{1,0:T(8,128)S(1)} %copy.48, f32[512,512]{1,0:T(8,128)} %collective-permute-done.2), kind=kLoop, calls=%fused_computation.46 | loop fusion | flops 524288 | bytes 2621440 | tf_op jit(solution)/shard_map/broadcast_in_dim | solution.py:154
  110.7 19.0 %all-reduce.2.cloned.1.call-done = bf16[32,1024]{1,0:T(8,128)(2,1)} async-done(((bf16[32,1024]{1,0:T(8,128)(2,1)}), bf16[32,1024]{1,0:T(8,128)(2,1)}) %all-reduce.2.cloned.1.call-update) | async-done | bytes 65552 | tf_op jit(solution)/shard_map/psum | solution.py:149
  129.6 1.5 %convert_multiply_fusion = f32[32,1024]{1,0:T(8,128)} fusion(bf16[32,1024]{1,0:T(8,128)(2,1)} %all-reduce.2.cloned.1.call-done), kind=kLoop, calls=%fused_computation.49 | loop fusion | flops 65536 | bytes 196608 | tf_op jit(solution)/shard_map/div | solution.py:151
  (7 shorter events, 0.0 us)
Async XLA Ops:
  7.2 29.6 %copy-start = (bf16[1,512,1024]{2,1,0:T(8,128)(2,1)S(1)}, bf16[1,512,1024]{2,1,0:T(8,128)(2,1)}, u32[]{:S(2)}) copy-start(bf16[1,512,1024]{2,1,0:T(8,128)(2,1)} %param.13) | copy-start | bytes 3145732
  7.2 13.5 %copy-start.6 = (bf16[1,512,512]{2,1,0:T(8,128)(2,1)S(1)}, bf16[1,512,512]{2,1,0:T(8,128)(2,1)}, u32[]{:S(2)}) copy-start(bf16[1,512,512]{2,1,0:T(8,128)(2,1)} %param.10) | copy-start | bytes 1572868
  7.2 13.7 %copy-start.9 = (s32[1,512]{1,0:T(1,128)S(1)}, s32[1,512]{1,0:T(1,128)}, u32[]{:S(2)}) copy-start(s32[1,512]{1,0:T(1,128)} %param.11) | copy-start | bytes 6148
  7.2 99.7 %reduce-scatter.2.cloned.1.call-start = ((), (), s32[]{:S(2)}) async-start(), calls=%async_computation.1 | async-start | bytes 2228224 | tf_op jit(solution)/shard_map/reduce_scatter | solution.py:141
  8.6 13.8 %collective-permute-start = (bf16[512,512]{0,1:T(8,128)(2,1)S(1)}, bf16[512,512]{0,1:T(8,128)(2,1)}, u32[]{:S(2)}, u32[]{:S(2)}) collective-permute-start(bf16[512,512]{0,1:T(8,128)(2,1)S(1)} %bitcast.106), channel_id=1, source_target_pairs={{0,1},{1,2},{2,3},{3,4},{4,5},{5,6},{6,7},{7,8},{8,9},{9,10},{10,1... | collective-permute-start | bytes 1572872 | tf_op jit(solution)/shard_map/ppermute | solution.py:16
  11.8 19.4 %collective-permute-start.1 = (bf16[512,512]{1,0:T(8,128)(2,1)}, bf16[512,512]{1,0:T(8,128)(2,1)}, u32[]{:S(2)}, u32[]{:S(2)}) collective-permute-start(bf16[512,512]{1,0:T(8,128)(2,1)} %bitcast.113), channel_id=1, source_target_pairs={{0,1},{1,2},{2,3},{3,4},{4,5},{5,6},{6,7},{7,8},{8,9},{9,10},{10,1... | collective-permute-start | bytes 1572872 | tf_op jit(solution)/shard_map/ppermute | solution.py:16
  20.7 10.6 %copy-start.4 = (bf16[1,512,512]{1,2,0:T(8,128)(2,1)}, bf16[1,512,512]{1,2,0:T(8,128)(2,1)S(1)}, u32[]{:S(2)}) copy-start(bf16[1,512,512]{1,2,0:T(8,128)(2,1)S(1)} %copy.62) | copy-start | bytes 1572868
  23.7 7.5 %copy-start.8 = (bf16[512,4,128]{2,0,1:T(8,128)(2,1)}, bf16[512,4,128]{2,0,1:T(8,128)(2,1)S(1)}, u32[]{:S(2)}) copy-start(bf16[512,4,128]{2,0,1:T(8,128)(2,1)S(1)} %copy.33) | copy-start | bytes 1572868
  23.8 9.6 %copy-start.7 = (bf16[1,512,512]{1,2,0:T(8,128)(2,1)S(1)}, bf16[1,512,512]{1,2,0:T(8,128)(2,1)}, u32[]{:S(2)}) copy-start(bf16[1,512,512]{1,2,0:T(8,128)(2,1)} %copy.36) | copy-start | bytes 1572868
  38.9 90.8 %all-reduce.2.cloned.1.call-start = ((), (), s32[]{:S(2)}) async-start(), calls=%async_computation.2 | async-start | bytes 131072 | tf_op jit(solution)/shard_map/psum | solution.py:149
  38.9 3.4 %copy-start.1 = (bf16[4,512,1024]{1,2,0:T(8,128)(2,1)S(1)}, bf16[4,512,1024]{1,2,0:T(8,128)(2,1)}, u32[]{:S(2)}) copy-start(bf16[4,512,1024]{1,2,0:T(8,128)(2,1)} %get-tuple-element.25) | copy-start | bytes 12582916
  42.3 1.7 %copy-start.3 = (bf16[512,512]{0,1:T(8,128)(2,1)}, bf16[512,512]{0,1:T(8,128)(2,1)S(1)}, u32[]{:S(2)}) copy-start(bf16[512,512]{0,1:T(8,128)(2,1)S(1)} %get-tuple-element.18) | copy-start | bytes 1572868
  45.5 24.4 %collective-permute-start.3 = (f32[512,512]{1,0:T(8,128)}, f32[512,512]{1,0:T(8,128)}, u32[]{:S(2)}, u32[]{:S(2)}) collective-permute-start(f32[512,512]{1,0:T(8,128)} %copy.50), channel_id=1, source_target_pairs={{1,0},{2,1},{3,2},{4,3},{5,4},{6,5},{7,6},{8,7},{9,8},{10,9},{11,1... | collective-permute-start | bytes 3145736 | tf_op jit(solution)/shard_map/ppermute | solution.py:16
  46.9 7.6 %copy-start.5 = (bf16[1,512,512]{1,2,0:T(8,128)(2,1)S(1)}, bf16[1,512,512]{1,2,0:T(8,128)(2,1)}, u32[]{:S(2)}) copy-start(bf16[1,512,512]{1,2,0:T(8,128)(2,1)} %copy-done.4) | copy-start | bytes 1572868
  54.5 2.6 %copy-start.2 = (bf16[4,512,1024]{1,2,0:T(8,128)(2,1)}, bf16[4,512,1024]{1,2,0:T(8,128)(2,1)S(1)}, u32[]{:S(2)}) copy-start(bf16[4,512,1024]{1,2,0:T(8,128)(2,1)S(1)} %fusion.10) | copy-start | bytes 12582916
  58.4 50.1 %collective-permute-start.2 = (f32[512,512]{1,0:T(8,128)}, f32[512,512]{1,0:T(8,128)}, u32[]{:S(2)}, u32[]{:S(2)}) collective-permute-start(f32[512,512]{1,0:T(8,128)} %copy.47), channel_id=1, source_target_pairs={{1,0},{2,1},{3,2},{4,3},{5,4},{6,5},{7,6},{8,7},{9,8},{10,9},{11,1... | collective-permute-start | bytes 3145736 | tf_op jit(solution)/shard_map/ppermute | solution.py:16
Sparse Core Ops, SparseCore 0:
  39.0 67.8 reduce-scatter.1
  109.7 19.8 all-reduce.1
where the time goes:
time: 139 us; the launch traced here: 138 us
  waiting for transfers between devices  53.9 us (39%)
  matrix products  29.4 us (21%)
  local copies, waits for them, and re-layouts  19.3 us (14%)
  between operations  14.3 us (10%)
  starting transfers between devices  10.6 us (8%)
  other arithmetic  10.5 us (8%)
    reduce_scatter x1, waiting for transfers between devices, shards(): lax.psum_scatter(lax.dot_general(hidden, grad_loc, (((0,), (0,)), ((), ()...  34.9 us
    psum x1, waiting for transfers between devices, shards(): lax.psum(weight_part.astype(jnp.bfloat16), 'dp').astype(jnp.float32)  19 us
    ppermute x4, starting transfers between devices, shifted(): lax.ppermute(value, axis, [(source, source + steps) for source in range(f...  10.5 us
    unnamed x25, local copies, waits for them, and re-layouts  7.78 us
    dot_general x1, matrix products, back_piece(): jnp.einsum('rhd,chd->hrc', split_heads(d_attn), split_heads(value_piece),...  7.53 us
    dot_general x1, matrix products, score_block(): jnp.einsum('rhd,chd->hrc', split_heads(query_rows), split_heads(key_piece...  7.48 us
    dot_general x1, matrix products, back_piece(): jnp.einsum('hrc,chd->rhd', d_scores, split_heads(key_piece), preferred_el...  4.12 us
    slice x4, local copies, waits for them, and re-layouts, shards(): remote_parts = [(key_part[0:tail], value_part[0:tail])]  4.07 us
  transfers between devices with their start and end apart: 6, of which 2 were waited for; matrix products, arithmetic and copies ran while one was open for 35% of the time, Pallas kernels for 0%

commit v1 on v0

--- a/solution.py
+++ b/solution.py
@@ -8,6 +8,11 @@
 HS = 128
 WIN = 512
 EPSILON = 1e-05
+
+
+def flows_take(a0):
+    tmp = jnp.sum(lax.all_gather(a0, "dp"), axis=0)
+    return tmp
 
 
 def shifted(value, axis, steps):
@@ -146,7 +151,7 @@
         scatter_dimension=0,
         tiled=True,
     )
-    weight_total = lax.psum(weight_part.astype(jnp.bfloat16), "dp").astype(jnp.float32)
+    weight_total = flows_take(weight_part.astype(jnp.bfloat16)).astype(jnp.float32)
     total_rows = lax.axis_size("dp") * hist_size * ev_rows
     weight_grad = weight_total / math.sqrt(total_rows)
     return (

time: 139 us -> 121 us (0.87)
  waiting for transfers between devices: 53.9 us -> 32.8 us
  blocking collectives: 0 us -> 4.93 us
  other arithmetic: 10.5 us -> 9.03 us
    psum x1 -> x0, waiting for transfers between devices: 19 us -> none  [shards(): lax.psum(weight_part.astype(jnp.bfloat16), 'dp').astype(jnp.float32)]
    all_gather x0 -> x1, blocking collectives: none -> 4.93 us  [flows_take(): tmp = jnp.sum(lax.all_gather(a0, 'dp'), axis=0)]
    reduce_scatter x1, waiting for transfers between devices: 34.9 us -> 32.7 us  [shards(): lax.psum_scatter(lax.dot_general(hidden, grad_loc, (((0,), (0,)), ((), ()...]
  transfers between devices with their start and end apart: 6 -> 5, of which waited for: 2 -> 1; matrix products, arithmetic and copies ran while one was open for 35% -> 39% of each run, Pallas kernels for 0% -> 0%
where the time goes in v1:
time: 121 us; the launch traced here: 120 us
  waiting for transfers between devices  32.8 us (27%)
  matrix products  29.4 us (24%)
  local copies, waits for them, and re-layouts  19.3 us (16%)
  between operations  14.3 us (12%)
  starting transfers between devices  10.5 us (9%)
  other arithmetic  9.03 us (7%)
  blocking collectives  4.93 us (4%)
    reduce_scatter x1, waiting for transfers between devices, shards(): lax.psum_scatter(lax.dot_general(hidden, grad_loc, (((0,), (0,)), ((), ()...  32.7 us
    ppermute x4, starting transfers between devices, shifted(): lax.ppermute(value, axis, [(source, source + steps) for source in range(f...  10.5 us
    unnamed x25, local copies, waits for them, and re-layouts  7.78 us
    dot_general x1, matrix products, back_piece(): jnp.einsum('rhd,chd->hrc', split_heads(d_attn), split_heads(value_piece),...  7.53 us
    dot_general x1, matrix products, score_block(): jnp.einsum('rhd,chd->hrc', split_heads(query_rows), split_heads(key_piece...  7.49 us
    all_gather x1, blocking collectives, flows_take(): tmp = jnp.sum(lax.all_gather(a0, 'dp'), axis=0)  4.93 us
    dot_general x1, matrix products, back_piece(): jnp.einsum('hrc,chd->rhd', d_scores, split_heads(key_piece), preferred_el...  4.12 us
    slice x4, local copies, waits for them, and re-layouts, shards(): remote_parts = [(key_part[0:tail], value_part[0:tail])]  4.05 us
  transfers between devices with their start and end apart: 5, of which 1 were waited for; matrix products, arithmetic and copies ran while one was open for 39% of the time, Pallas kernels for 0%

profile of v1, /device:TPU:0, one launch (start us, length us, event | category | flops | bytes accessed | tf_op | source)
XLA Modules:
  0.0 120.3 jit_solution(11984075190738245557)
XLA Ops:
  7.2 0.0 copy-start
  7.2 0.0 copy-start.6
  7.2 0.0 copy-start.9
  7.2 0.0 reduce-scatter.2.cloned.1.call-start
  7.2 1.4 %copy.31 = bf16[1,512,512]{1,2,0:T(8,128)(2,1)S(1)} copy(bf16[1,512,512]{2,1,0:T(8,128)(2,1)} %param.8) | data formatting | bytes 1048576 | tf_op args[1]
  8.6 3.2 %collective-permute-start = (bf16[512,512]{0,1:T(8,128)(2,1)S(1)}, bf16[512,512]{0,1:T(8,128)(2,1)}, u32[]{:S(2)}, u32[]{:S(2)}) collective-permute-start(bf16[512,512]{0,1:T(8,128)(2,1)S(1)} %bitcast.107), channel_id=1, source_target_pairs={{0,1},{1,2},{2,3},{3,4},{4,5},{5,6},{6,7},{7,8},{8,9},{9,10},{10,1... | collective-permute-start | bytes 1572872 | tf_op jit(solution)/shard_map/ppermute | solution.py:21
  11.8 4.5 %collective-permute-start.1 = (bf16[512,512]{1,0:T(8,128)(2,1)}, bf16[512,512]{1,0:T(8,128)(2,1)}, u32[]{:S(2)}, u32[]{:S(2)}) collective-permute-start(bf16[512,512]{1,0:T(8,128)(2,1)} %bitcast.115), channel_id=1, source_target_pairs={{0,1},{1,2},{2,3},{3,4},{4,5},{5,6},{6,7},{7,8},{8,9},{9,10},{10,1... | collective-permute-start | bytes 1572872 | tf_op jit(solution)/shard_map/ppermute | solution.py:21
  16.4 2.0 %copy.36 = bf16[1,512,512]{1,2,0:T(8,128)(2,1)} copy(bf16[1,512,512]{2,1,0:T(8,128)(2,1)} %param.9) | data formatting | bytes 1048576 | tf_op args[2]
  18.4 1.0 copy.34
  19.4 1.3 %copy.62 = bf16[1,512,512]{1,2,0:T(8,128)(2,1)S(1)} copy(bf16[1,512,512]{2,1,0:T(8,128)(2,1)} %param.7) | data formatting | bytes 1048576 | tf_op jit(solution)/shard_map/reshape;squeeze | solution.py:25
  20.7 0.0 copy-done.6
  20.7 0.0 copy-start.4
  20.7 0.2 copy.39
  20.9 0.0 copy-done.9
  20.9 0.7 fusion.18
  21.6 0.8 pad_add_fusion
  22.4 0.0 collective-permute-done
  22.4 1.3 %copy.33 = bf16[512,4,128]{2,0,1:T(8,128)(2,1)S(1)} copy(bf16[512,4,128]{0,2,1:T(8,128)(2,1)} %bitcast.1) | data formatting | bytes 1048576 | tf_op jit(solution)/shard_map/concatenate | solution.py:128
  23.7 0.0 copy-start.8
  23.8 0.0 copy-start.7
  23.8 7.5 %fusion.5 = (bf16[4,512,1024]{1,2,0:T(8,128)(2,1)}, f32[4,1024,512]{2,1,0:T(8,128)}) fusion(pred[512,1024]{0,1:T(8,128)(4,1)} %pad_add_fusion, bf16[512,4,128]{0,2,1:T(8,128)(2,1)S(1)} %bitcast.112, bf16[512,4,128]{2,0,1:T(8,128)(2,1)} %copy.34, bf16[512,4,128]{2,0,1:T(8,128)(2,1)S(1)} %copy.33), kind=kOutput, calls=%fused_computation.8 | convolution fusion | flops 555745280 | bytes 14680064 | tf_op jit(solution)/shard_map/rhd,chd->hrc/dot_general | solution.py:29
  31.3 0.0 copy-done.4
  31.3 0.0 copy-done.8
  31.3 0.0 collective-permute-done.1
  31.3 2.0 %copy.35 = bf16[512,512]{0,1:T(8,128)(2,1)} copy(bf16[512,512]{1,0:T(8,128)(2,1)} %collective-permute-done.1) | data formatting | bytes 1048576 | tf_op jit(solution)/shard_map/ppermute | solution.py:21
  33.3 0.0 copy-done.7
  33.3 3.1 %fusion.32 = (f32[512]{0:T(512)S(1)}, f32[4,128,512]{2,1,0:T(8,128)S(1)}) fusion(bf16[4,512,1024]{1,2,0:T(8,128)(2,1)} %get-tuple-element.25, bf16[512,4,128]{0,2,1:T(8,128)(2,1)S(1)} %bitcast.117, bf16[512,4,128]{0,2,1:T(8,128)(2,1)} %bitcast.118), kind=kOutput, calls=%fused_computation.62 | convolution fusion | flops 539229696 | bytes 6293504 | tf_op jit(solution)/shard_map/hrc,chd->rhd/dot_general | solution.py:52
  36.4 0.2 multiply_reduce_fusion.1
  36.6 0.2 multiply_convert_fusion
  36.8 0.0 copy-done
  36.8 2.0 %fusion.13 = f32[512,1024]{1,0:T(8,128)} fusion(bf16[512,512]{0,1:T(8,128)(2,1)S(1)} %bitcast.109, bf16[1,512,1024]{2,1,0:T(8,128)(2,1)S(1)} %copy-done), kind=kOutput, calls=%fused_computation.28 | convolution fusion | flops 536870912 | bytes 3670016 | tf_op jit(solution)/shard_map/dot_general | solution.py:147
  38.9 0.0 reduce-scatter.2.cloned.1.call-update
  38.9 0.0 copy-start.1
  38.9 2.2 %fusion.25 = (f32[512]{0:T(512)S(1)}, f32[512]{0:T(512)S(1)}, f32[512,512]{0,1:T(8,128)S(1)}) fusion(bf16[1,512,512]{1,2,0:T(8,128)(2,1)S(1)} %copy.39, f32[512]{0:T(512)S(1)} %add_rsqrt_fusion, f32[512]{0:T(512)S(1)} %broadcast_multiply_fusion.2, f32[4,128,512]{2,1,0:T(8,128)S(1)} %get-tuple-element.28, bf16[512,1024]{1,0:T(8,128)(2,1)} %param.12, ...), kind=kOutput, calls=%fused_computation.48 | convolution fusion | flops 538704896 | bytes 4726784 | tf_op jit(solution)/shard_map/dot_general | solution.py:95
  41.1 1.2 multiply_convert_fusion.1
  42.3 0.0 copy-start.3
  42.3 0.0 copy-done.1
  42.3 1.5 %convolution_bitcast_fusion = f32[1024,4,128]{0,2,1:T(8,128)S(1)} fusion(bf16[512,4,128]{0,2,1:T(8,128)(2,1)S(1)} %bitcast.110, bf16[4,512,1024]{1,2,0:T(8,128)(2,1)S(1)} %copy-done.1), kind=kOutput, calls=%fused_computation.16 | convolution fusion | flops 536870912 | bytes 6815744 | tf_op jit(solution)/shard_map/hrc,rhd->chd/dot_general | solution.py:80
  43.8 0.2 fusion.30
  44.0 0.0 copy-done.3
  44.0 1.4 %copy.50 = f32[512,512]{1,0:T(8,128)} copy(f32[512,512]{0,1:T(8,128)S(1)} %bitcast.104) | data formatting | bytes 2097152 | tf_op jit(solution)/shard_map/slice | solution.py:139
  45.4 1.5 %collective-permute-start.3 = (f32[512,512]{1,0:T(8,128)}, f32[512,512]{1,0:T(8,128)}, u32[]{:S(2)}, u32[]{:S(2)}) collective-permute-start(f32[512,512]{1,0:T(8,128)} %copy.50), channel_id=1, source_target_pairs={{1,0},{2,1},{3,2},{4,3},{5,4},{6,5},{7,6},{8,7},{9,8},{10,9},{11,1... | collective-permute-start | bytes 3145736 | tf_op jit(solution)/shard_map/ppermute | solution.py:21
  46.9 0.0 copy-start.5
  46.9 7.5 %fusion.10 = bf16[4,512,1024]{1,2,0:T(8,128)(2,1)S(1)} fusion(f32[4,1024,512]{2,1,0:T(8,128)} %get-tuple-element.26, pred[512,1024]{0,1:T(8,128)(4,1)} %pad_add_fusion, bf16[512,4,128]{0,2,1:T(8,128)(2,1)} %bitcast.111, bf16[512,4,128]{0,2,1:T(8,128)(2,1)} %bitcast.116, bf16[512,4,128]{0,2,1:T(8,128)(2,1)} %bitcast.119), kind=kOutput, calls=%fused_computation.13 | convolution fusion | flops 564133888 | bytes 14680064 | tf_op jit(solution)/shard_map/rhd,chd->hrc/dot_general | solution.py:62
  54.4 0.0 copy-done.5
  54.4 0.0 copy-start.2
  54.4 1.5 %multiply_bitcast_fusion = f32[1024,4,128]{0,2,1:T(8,128)S(1)} fusion(bf16[4,512,1024]{1,2,0:T(8,128)(2,1)S(1)} %fusion.10, bf16[512,4,128]{0,2,1:T(8,128)(2,1)S(1)} %bitcast.113), kind=kOutput, calls=%fused_computation.14 | convolution fusion | flops 537395200 | bytes 6815744 | tf_op jit(solution)/shard_map/hrc,rhd->chd/dot_general | solution.py:77
  55.9 1.1 fusion.31
  57.1 0.0 copy-done.2
  57.1 1.3 %copy.47 = f32[512,512]{1,0:T(8,128)} copy(f32[512,512]{0,1:T(8,128)S(1)} %bitcast.105) | data formatting | bytes 2097152 | tf_op jit(solution)/shard_map/slice | solution.py:139
  58.4 1.3 %collective-permute-start.2 = (f32[512,512]{1,0:T(8,128)}, f32[512,512]{1,0:T(8,128)}, u32[]{:S(2)}, u32[]{:S(2)}) collective-permute-start(f32[512,512]{1,0:T(8,128)} %copy.47), channel_id=1, source_target_pairs={{1,0},{2,1},{3,2},{4,3},{5,4},{6,5},{7,6},{8,7},{9,8},{10,9},{11,1... | collective-permute-start | bytes 3145736 | tf_op jit(solution)/shard_map/ppermute | solution.py:21
  59.7 0.3 copy.51
  60.0 1.6 %copy.48 = f32[512,512]{1,0:T(8,128)S(1)} copy(f32[512,512]{0,1:T(8,128)} %bitcast.103) | data formatting | bytes 2097152 | tf_op jit(solution)/shard_map/slice | solution.py:137
  61.6 4.1 %fusion.11 = bf16[4,128,512]{2,1,0:T(8,128)(2,1)} fusion(bf16[4,512,1024]{1,2,0:T(8,128)(2,1)} %copy-done.2, bf16[512,4,128]{2,0,1:T(8,128)(2,1)} %copy.34, bf16[512,4,128]{2,0,1:T(8,128)(2,1)} %copy-done.8), kind=kOutput, calls=%fused_computation.22 | convolution fusion | flops 539492352 | bytes 5767168 | tf_op jit(solution)/shard_map/hrc,chd->rhd/dot_general | solution.py:73
  65.7 2.1 %copy.52 = bf16[1,512,512]{2,1,0:T(8,128)(2,1)} copy(bf16[1,512,512]{1,2,0:T(8,128)(2,1)} %bitcast.120) | data formatting | bytes 1048576
  67.8 2.0 %copy.53 = bf16[1,512,512]{2,1,0:T(8,128)(2,1)} copy(bf16[1,512,512]{1,2,0:T(8,128)(2,1)} %bitcast.106) | data formatting | bytes 1048576
  69.8 0.0 collective-permute-done.3
  69.8 2.2 %fusion.24 = bf16[1,512,512]{2,1,0:T(8,128)(2,1)} fusion(f32[512,512]{1,0:T(8,128)S(1)} %copy.51, f32[512,512]{1,0:T(8,128)} %collective-permute-done.3), kind=kLoop, calls=%fused_computation.47 | loop fusion | flops 524288 | bytes 2621440 | tf_op jit(solution)/shard_map/broadcast_in_dim | solution.py:160
  72.0 0.0 collective-permute-done.2
  72.0 2.2 %fusion.23 = bf16[1,512,512]{2,1,0:T(8,128)(2,1)} fusion(f32[512,512]{1,0:T(8,128)S(1)} %copy.48, f32[512,512]{1,0:T(8,128)} %collective-permute-done.2), kind=kLoop, calls=%fused_computation.46 | loop fusion | flops 524288 | bytes 2621440 | tf_op jit(solution)/shard_map/broadcast_in_dim | solution.py:159
  74.2 32.7 %reduce-scatter.2.cloned.1.call-done = f32[32,1024]{1,0:T(8,128)} async-done(((f32[512,1024]{1,0:T(8,128)}), f32[32,1024]{1,0:T(8,128)}) %reduce-scatter.2.cloned.1.call-update) | async-done | bytes 131088 | tf_op jit(solution)/shard_map/reduce_scatter | solution.py:146
  106.9 0.9 convert_element_type.76
  107.8 4.9 %all-gather = bf16[64,1024]{1,0:T(8,128)(2,1)S(1)} all-gather(bf16[32,1024]{1,0:T(8,128)(2,1)S(1)} %convert_element_type.76), channel_id=2, replica_groups=mesh['dp'=2,'hist'=16] {'dp'}, dimensions={0}, use_global_device_ids=true | all-gather | bytes 196608 | tf_op jit(solution)/shard_map/all_gather | solution.py:14
  112.8 0.7 convert_multiply_fusion
  (6 shorter events, 0.1 us)
Async XLA Ops:
  7.2 29.7 %copy-start = (bf16[1,512,1024]{2,1,0:T(8,128)(2,1)S(1)}, bf16[1,512,1024]{2,1,0:T(8,128)(2,1)}, u32[]{:S(2)}) copy-start(bf16[1,512,1024]{2,1,0:T(8,128)(2,1)} %param.13) | copy-start | bytes 3145732
  7.2 13.5 %copy-start.6 = (bf16[1,512,512]{2,1,0:T(8,128)(2,1)S(1)}, bf16[1,512,512]{2,1,0:T(8,128)(2,1)}, u32[]{:S(2)}) copy-start(bf16[1,512,512]{2,1,0:T(8,128)(2,1)} %param.10) | copy-start | bytes 1572868
  7.2 13.7 %copy-start.9 = (s32[1,512]{1,0:T(1,128)S(1)}, s32[1,512]{1,0:T(1,128)}, u32[]{:S(2)}) copy-start(s32[1,512]{1,0:T(1,128)} %param.11) | copy-start | bytes 6148
  7.2 99.7 %reduce-scatter.2.cloned.1.call-start = ((), (), s32[]{:S(2)}) async-start(), calls=%async_computation.1 | async-start | bytes 2228224 | tf_op jit(solution)/shard_map/reduce_scatter | solution.py:146
  8.6 13.8 %collective-permute-start = (bf16[512,512]{0,1:T(8,128)(2,1)S(1)}, bf16[512,512]{0,1:T(8,128)(2,1)}, u32[]{:S(2)}, u32[]{:S(2)}) collective-permute-start(bf16[512,512]{0,1:T(8,128)(2,1)S(1)} %bitcast.107), channel_id=1, source_target_pairs={{0,1},{1,2},{2,3},{3,4},{4,5},{5,6},{6,7},{7,8},{8,9},{9,10},{10,1... | collective-permute-start | bytes 1572872 | tf_op jit(solution)/shard_map/ppermute | solution.py:21
  11.8 19.5 %collective-permute-start.1 = (bf16[512,512]{1,0:T(8,128)(2,1)}, bf16[512,512]{1,0:T(8,128)(2,1)}, u32[]{:S(2)}, u32[]{:S(2)}) collective-permute-start(bf16[512,512]{1,0:T(8,128)(2,1)} %bitcast.115), channel_id=1, source_target_pairs={{0,1},{1,2},{2,3},{3,4},{4,5},{5,6},{6,7},{7,8},{8,9},{9,10},{10,1... | collective-permute-start | bytes 1572872 | tf_op jit(solution)/shard_map/ppermute | solution.py:21
  20.7 10.6 %copy-start.4 = (bf16[1,512,512]{1,2,0:T(8,128)(2,1)}, bf16[1,512,512]{1,2,0:T(8,128)(2,1)S(1)}, u32[]{:S(2)}) copy-start(bf16[1,512,512]{1,2,0:T(8,128)(2,1)S(1)} %copy.62) | copy-start | bytes 1572868
  23.7 7.5 %copy-start.8 = (bf16[512,4,128]{2,0,1:T(8,128)(2,1)}, bf16[512,4,128]{2,0,1:T(8,128)(2,1)S(1)}, u32[]{:S(2)}) copy-start(bf16[512,4,128]{2,0,1:T(8,128)(2,1)S(1)} %copy.33) | copy-start | bytes 1572868
  23.8 9.6 %copy-start.7 = (bf16[1,512,512]{1,2,0:T(8,128)(2,1)S(1)}, bf16[1,512,512]{1,2,0:T(8,128)(2,1)}, u32[]{:S(2)}) copy-start(bf16[1,512,512]{1,2,0:T(8,128)(2,1)} %copy.36) | copy-start | bytes 1572868
  38.9 3.4 %copy-start.1 = (bf16[4,512,1024]{1,2,0:T(8,128)(2,1)S(1)}, bf16[4,512,1024]{1,2,0:T(8,128)(2,1)}, u32[]{:S(2)}) copy-start(bf16[4,512,1024]{1,2,0:T(8,128)(2,1)} %get-tuple-element.25) | copy-start | bytes 12582916
  42.3 1.7 %copy-start.3 = (bf16[512,512]{0,1:T(8,128)(2,1)}, bf16[512,512]{0,1:T(8,128)(2,1)S(1)}, u32[]{:S(2)}) copy-start(bf16[512,512]{0,1:T(8,128)(2,1)S(1)} %get-tuple-element.18) | copy-start | bytes 1572868
  45.4 24.4 %collective-permute-start.3 = (f32[512,512]{1,0:T(8,128)}, f32[512,512]{1,0:T(8,128)}, u32[]{:S(2)}, u32[]{:S(2)}) collective-permute-start(f32[512,512]{1,0:T(8,128)} %copy.50), channel_id=1, source_target_pairs={{1,0},{2,1},{3,2},{4,3},{5,4},{6,5},{7,6},{8,7},{9,8},{10,9},{11,1... | collective-permute-start | bytes 3145736 | tf_op jit(solution)/shard_map/ppermute | solution.py:21
  46.9 7.6 %copy-start.5 = (bf16[1,512,512]{1,2,0:T(8,128)(2,1)S(1)}, bf16[1,512,512]{1,2,0:T(8,128)(2,1)}, u32[]{:S(2)}) copy-start(bf16[1,512,512]{1,2,0:T(8,128)(2,1)} %copy-done.4) | copy-start | bytes 1572868
  54.4 2.6 %copy-start.2 = (bf16[4,512,1024]{1,2,0:T(8,128)(2,1)}, bf16[4,512,1024]{1,2,0:T(8,128)(2,1)S(1)}, u32[]{:S(2)}) copy-start(bf16[4,512,1024]{1,2,0:T(8,128)(2,1)S(1)} %fusion.10) | copy-start | bytes 12582916
  58.4 13.6 %collective-permute-start.2 = (f32[512,512]{1,0:T(8,128)}, f32[512,512]{1,0:T(8,128)}, u32[]{:S(2)}, u32[]{:S(2)}) collective-permute-start(f32[512,512]{1,0:T(8,128)} %copy.47), channel_id=1, source_target_pairs={{1,0},{2,1},{3,2},{4,3},{5,4},{6,5},{7,6},{8,7},{9,8},{10,9},{11,1... | collective-permute-start | bytes 3145736 | tf_op jit(solution)/shard_map/ppermute | solution.py:21
Sparse Core Ops, SparseCore 0:
  39.0 67.8 reduce-scatter.1
